TPU v7x, 512 devices: a whole 4x4x16 slice. The times are simulated.
512 devices in a mesh: section: 16 (over z), expert: 8 (over y, core), dp: 4 (over x).
Axes of the slice: x: 4, y: 4, z: 16, core: 2. Of those that a mesh axis runs over, the one named last changes fastest.
Arguments:
- tokens: bfloat16 [1024, 3072], P('expert', 'dp'), may hold values from -6 to 6
- expert_ids: int32 [1024, 2], P('expert'), may hold values from 0 to 7, all different within a row; in each aligned block of 128 rows (0 to 127, 128 to 255, ...) at most 64 rows name the same one
- w_gate: bfloat16 [8, 3072, 8192], P('expert', 'dp', 'section'), may hold values from -0.109375 to 0.109375
- w_up: bfloat16 [8, 3072, 8192], P('expert', 'dp', 'section'), may hold values from -0.109375 to 0.109375
- cotangent: bfloat16 [8, 512, 8192], P('expert', None, 'section'), may hold values from -6 to 6
Outputs:
- acted: bfloat16 [8, 512, 8192], P('expert', None, 'section')
- input_grad: bfloat16 [1024, 3072], P('expert', 'dp')
- gate_grad: bfloat16 [8, 3072, 8192], P('expert', 'dp', 'section')
- up_grad: bfloat16 [8, 3072, 8192], P('expert', 'dp', 'section')
Inputs may be any that keep to these rules, and one draw needn't show every extreme that they name: `expert_ids`: each token names two different experts. Among the 128 tokens of one index of the expert axis no expert is named more than 64 times, a bound that some block reaches.
All inputs are finite; a program needn't handle non-finite values.
Results may differ from a plain program's by a relative error of at most 0.0049.
Values may be sent and summed in bfloat16 or wider, within the bound.
A program may use at most 64 MiB of HBM per device.

v0:
```python
import jax
import jax.numpy as jnp
from jax import lax
from jax.sharding import PartitionSpec as P


def local(tokens, expert_ids, w_gate, w_up, cotangent):
    rows, width = tokens.shape
    experts = lax.axis_size("expert")
    capacity = min(rows, 4 * rows // experts)
    wg = w_gate[0]
    wu = w_up[0]
    flat_ids = expert_ids.reshape(-1)
    member = (flat_ids[:, None] == jnp.arange(experts, dtype=jnp.int32)[None, :]).astype(jnp.int32)
    rank = jnp.sum((jnp.cumsum(member, axis=0) - member) * member, axis=1)
    slot = flat_ids * capacity + rank
    token_of = jnp.arange(2 * rows, dtype=jnp.int32) // 2
    source = jnp.full((experts * capacity,), rows, jnp.int32).at[slot].set(token_of)
    occupied = jnp.zeros((experts * capacity,), jnp.bfloat16).at[slot].set(1.0)
    x_pad = jnp.concatenate([tokens, jnp.zeros((1, width), jnp.bfloat16)], axis=0)
    send_x = jnp.take(x_pad, source, axis=0).reshape(experts, capacity, width)
    recv_x, recv_live = (
        lax.all_to_all(send_x, "expert", split_axis=0, concat_axis=0, tiled=True),
        lax.all_to_all(
            occupied.reshape(experts, capacity), "expert", split_axis=0, concat_axis=0, tiled=True
        ),
    )
    x_rows = recv_x.reshape(-1, width)
    parts = (x_rows,)
    part_gate = jnp.dot(parts[0], wg, preferred_element_type=jnp.float32)
    part_up = jnp.dot(parts[0], wu, preferred_element_type=jnp.float32)
    pre_gate, pre_up = lax.psum((part_gate, part_up), "dp")
    sig = jax.nn.sigmoid(pre_gate)
    silu_v = pre_gate * sig
    acted = (silu_v * pre_up).astype(jnp.bfloat16)
    cf = cotangent[0].astype(jnp.float32)
    gate_part = (cf * pre_up * sig * (1.0 + pre_gate * (1.0 - sig))).astype(jnp.bfloat16)
    up_part = (cf * silu_v).astype(jnp.bfloat16)
    contract = (((0,), (0,)), ((), ()))
    gate_grad = lax.dot_general(x_rows, gate_part, contract, preferred_element_type=jnp.float32)
    up_grad = lax.dot_general(x_rows, up_part, contract, preferred_element_type=jnp.float32)
    parts = (gate_part, up_part)
    back = lax.dot_general(
        parts[0], wg, (((1,), (1,)), ((), ())), preferred_element_type=jnp.float32
    ) + lax.dot_general(parts[1], wu, (((1,), (1,)), ((), ())), preferred_element_type=jnp.float32)
    back = (back,)[0]
    whole = lax.psum(back, "section")
    home = lax.all_to_all(
        whole.reshape(experts, capacity, width), "expert", split_axis=0, concat_axis=0, tiled=True
    )
    token_grad = jnp.sum(
        jnp.take(home.reshape(-1, width), slot, axis=0).reshape(rows, 2, width), axis=1
    )
    return (
        acted[None],
        token_grad.astype(jnp.bfloat16),
        gate_grad.astype(jnp.bfloat16)[None],
        up_grad.astype(jnp.bfloat16)[None],
    )


def solution(mesh):
    placed = (
        P("expert", "dp"),
        P("expert", None),
        P("expert", "dp", "section"),
        P("expert", "dp", "section"),
        P("expert", None, "section"),
    )
    return jax.shard_map(
        local,
        mesh=mesh,
        in_specs=placed,
        out_specs=(
            P("expert", None, "section"),
            P("expert", "dp"),
            P("expert", "dp", "section"),
            P("expert", "dp", "section"),
        ),
        check_vma=False,
    )
```

profile of v0, /device:TPU:1, one launch (start us, length us, event | category | flops | bytes accessed | tf_op | source)
XLA Modules:
  0.0 297.3 jit_solution(851770255115678732)
XLA Ops:
  7.2 0.7 broadcast_multiply_fusion
  8.0 0.8 copy.14
  9.3 0.6 reduce-window.6
  9.9 0.2 slice_reduce_fusion
  10.3 1.4 scatter_custom_fusion
  11.8 0.9 concatenate.3
  12.7 2.0 gather_fusion
  14.9 21.5 %all_to_all.10 = bf16[8,64,768]{2,1,0:T(8,128)(2,1)S(1)} all-to-all(bf16[8,64,768]{2,1,0:T(8,128)(2,1)S(1)} %broadcast_select_fusion), channel_id=1, replica_groups=mesh['section'=16,'expert'=8,'dp'=4] {'expert'}, dimensions={0} | all-to-all | bytes 1572864 | tf_op jit(solution)/shard_map/all_to_all | solution.py:23
  36.4 1.6 fusion.8
  38.1 1.6 fusion.12
  39.7 73.3 %all-reduce.7.cloned.1.call-done = (f32[512,512]{1,0:T(8,128)}, f32[512,512]{1,0:T(8,128)}) async-done(((f32[512,512]{1,0:T(8,128)}, f32[512,512]{1,0:T(8,128)}), (f32[512,512]{1,0:T(8,128)}, f32[512,512]{1,0:T(8,128)})) %all-reduce.7.cloned.1.call-update) | async-done | bytes 2097168 | tf_op jit(solution)/shard_map/psum | solution.py:32
  113.0 2.9 fusion.4
  115.9 0.6 fusion.10
  116.5 0.8 copy-done.2
  117.3 0.2 copy-done.5
  117.7 1.9 convolution_add_fusion
  119.7 132.2 %all-reduce.5.cloned.1.call-done = f32[8,64,768]{2,1,0:T(8,128)} async-done(((f32[8,64,768]{2,1,0:T(8,128)}), f32[8,64,768]{2,1,0:T(8,128)}) %all-reduce.5.cloned.1.call-update) | async-done | bytes 1572880 | tf_op jit(solution)/shard_map/psum | solution.py:47
  251.8 14.7 %all-to-all-start.1 = ((f32[8,64,768]{2,1,0:T(8,128)}), f32[8,64,768]{2,1,0:T(8,128)S(1)}, u32[]{:S(2)}, u32[]{:S(2)}) async-start(f32[8,64,768]{2,1,0:T(8,128)} %all-reduce.5.cloned.1.call-done), calls=%async_computation.1 | async-start | bytes 3145728 | tf_op jit(solution)/shard_map/all_to_all | solution.py:48
  266.9 2.6 fusion
  269.6 1.6 fusion.1
  271.2 15.9 %all-to-all-done.1 = f32[8,64,768]{2,1,0:T(8,128)S(1)} async-done(((f32[8,64,768]{2,1,0:T(8,128)}), f32[8,64,768]{2,1,0:T(8,128)S(1)}, u32[]{:S(2)}, u32[]{:S(2)}) %all-to-all-start.1) | async-done | bytes 1572896 | tf_op jit(solution)/shard_map/all_to_all | solution.py:48
  287.1 1.1 gather_fusion.1
  288.2 0.5 gather.15
  288.7 1.8 select_reduce_fusion
  (42 shorter events, 1.6 us)
Async XLA Ops:
  7.2 30.9 %copy-start = (bf16[1,768,512]{2,1,0:T(8,128)(2,1)S(1)}, bf16[1,768,512]{2,1,0:T(8,128)(2,1)}, u32[]{:S(2)}) copy-start(bf16[1,768,512]{2,1,0:T(8,128)(2,1)} %param.7) | copy-start | bytes 2359300
  7.2 105.8 %all-reduce.7.cloned.1.call-start = ((), (), s32[]{:S(2)}) async-start(), calls=%async_computation.3 | async-start | bytes 4194304 | tf_op jit(solution)/shard_map/psum | solution.py:32
  14.8 21.7 %copy-start.4 = (bf16[1,768,512]{2,1,0:T(8,128)(2,1)S(1)}, bf16[1,768,512]{2,1,0:T(8,128)(2,1)}, u32[]{:S(2)}) copy-start(bf16[1,768,512]{2,1,0:T(8,128)(2,1)} %param.8) | copy-start | bytes 2359300
  39.6 73.4 %copy-start.6 = (bf16[1,512,512]{2,1,0:T(8,128)(2,1)S(1)}, bf16[1,512,512]{2,1,0:T(8,128)(2,1)}, u32[]{:S(2)}) copy-start(bf16[1,512,512]{2,1,0:T(8,128)(2,1)} %param.9) | copy-start | bytes 1572868
  39.6 212.2 %all-reduce.5.cloned.1.call-start = ((), (), s32[]{:S(2)}) async-start(), calls=%async_computation.2 | async-start | bytes 3145728 | tf_op jit(solution)/shard_map/psum | solution.py:47
  115.9 3.7 %copy-start.1 = (bf16[512,512]{1,0:T(8,128)(2,1)}, bf16[512,512]{1,0:T(8,128)(2,1)S(1)}, u32[]{:S(2)}) copy-start(bf16[512,512]{1,0:T(8,128)(2,1)S(1)} %get-tuple-element.6) | copy-start | bytes 1572868
  115.9 1.4 copy-start.2
  115.9 1.6 copy-start.5
  115.9 1.8 copy-start.7
  119.6 147.1 %copy-start.9 = (s32[128,2]{0,1:T(2,128)S(1)}, s32[128,2]{0,1:T(2,128)}, u32[]{:S(2)}) copy-start(s32[128,2]{0,1:T(2,128)} %param.6) | copy-start | bytes 3076
  251.8 35.3 %all-to-all-start.1 = ((f32[8,64,768]{2,1,0:T(8,128)}), f32[8,64,768]{2,1,0:T(8,128)S(1)}, u32[]{:S(2)}, u32[]{:S(2)}) async-start(f32[8,64,768]{2,1,0:T(8,128)} %all-reduce.5.cloned.1.call-done), calls=%async_computation.1 | async-start | bytes 3145728 | tf_op jit(solution)/shard_map/all_to_all | solution.py:48
  266.9 2.7 copy-start.3
  266.9 2.7 copy-start.8
Sparse Core Ops, SparseCore 0:
  39.8 73.2 all-reduce.6
  119.8 132.0 all-reduce.4
where the time goes:
time: 298 us; the launch traced here: 297 us
  waiting for transfers between devices  221 us (74%)
  blocking collectives  21.5 us (7%)
  starting transfers between devices  14.8 us (5%)
  between operations  14.2 us (5%)
  matrix products  9.94 us (3%)
  local copies, waits for them, and re-layouts  9.07 us (3%)
  other arithmetic  6.29 us (2%)
    psum x1, waiting for transfers between devices, local(): whole = lax.psum(back, 'section')  132 us
    psum x1, waiting for transfers between devices, local(): pre_gate, pre_up = lax.psum((part_gate, part_up), 'dp')  73.3 us
    all_to_all x1, blocking collectives, local(): lax.all_to_all(send_x, 'expert', split_axis=0, concat_axis=0, tiled=True)  21.5 us
    all_to_all x1, waiting for transfers between devices, local(): lax.all_to_all(whole.reshape(experts, capacity, width), 'expert', split_a...  15.9 us
    all_to_all x1, starting transfers between devices, local(): lax.all_to_all(whole.reshape(experts, capacity, width), 'expert', split_a...  14.7 us
  transfers between devices with their start and end apart: 3, of which 3 were waited for; matrix products, arithmetic and copies ran while one was open for 2% of the time, Pallas kernels for 0%

commit v1 on v0

--- a/solution.py
+++ b/solution.py
@@ -44,7 +44,7 @@
         parts[0], wg, (((1,), (1,)), ((), ())), preferred_element_type=jnp.float32
     ) + lax.dot_general(parts[1], wu, (((1,), (1,)), ((), ())), preferred_element_type=jnp.float32)
     back = (back,)[0]
-    whole = lax.psum(back, "section")
+    whole = jnp.sum(lax.all_gather(back, axis_name="section"), 0)
     home = lax.all_to_all(
         whole.reshape(experts, capacity, width), "expert", split_axis=0, concat_axis=0, tiled=True
     )

time: 298 us -> 443 us (1.49)
  waiting for transfers between devices: 221 us -> 364 us
  other arithmetic: 6.29 us -> 17 us
  starting transfers between devices: 14.8 us -> 5.34 us
    all_gather x0 -> x1, waiting for transfers between devices: none -> 274 us  [local(): whole = jnp.sum(lax.all_gather(back, axis_name='section'), 0)]
    psum x1 -> x0, waiting for transfers between devices: 132 us -> none  [local(): whole = lax.psum(back, 'section')]
    reduce_sum x0 -> x1, other arithmetic: none -> 10.7 us  [local(): whole = jnp.sum(lax.all_gather(back, axis_name='section'), 0)]
    all_to_all x1, starting transfers between devices: 14.7 us -> 5.26 us  [local(): lax.all_to_all(whole.reshape(experts, capacity, width), 'expert', split_a...]
  transfers between devices with their start and end apart: 3 -> 3, of which waited for: 3 -> 3; matrix products, arithmetic and copies ran while one was open for 2% -> 1% of each run, Pallas kernels for 0% -> 0%
where the time goes in v1:
time: 443 us; the launch traced here: 442 us
  waiting for transfers between devices  364 us (82%)
  blocking collectives  21.5 us (5%)
  other arithmetic  17 us (4%)
  between operations  14.2 us (3%)
  local copies, waits for them, and re-layouts  10.7 us (2%)
  matrix products  10 us (2%)
  starting transfers between devices  5.34 us (1%)
    all_gather x1, waiting for transfers between devices, local(): whole = jnp.sum(lax.all_gather(back, axis_name='section'), 0)  274 us
    psum x1, waiting for transfers between devices, local(): pre_gate, pre_up = lax.psum((part_gate, part_up), 'dp')  73.3 us
    all_to_all x1, blocking collectives, local(): lax.all_to_all(send_x, 'expert', split_axis=0, concat_axis=0, tiled=True)  21.5 us
    all_to_all x1, waiting for transfers between devices, local(): lax.all_to_all(whole.reshape(experts, capacity, width), 'expert', split_a...  15.9 us
    reduce_sum x1, other arithmetic, local(): whole = jnp.sum(lax.all_gather(back, axis_name='section'), 0)  10.7 us
  transfers between devices with their start and end apart: 3, of which 3 were waited for; matrix products, arithmetic and copies ran while one was open for 1% of the time, Pallas kernels for 0%

profile of v1, /device:TPU:1, one launch (start us, length us, event | category | flops | bytes accessed | tf_op | source)
XLA Modules:
  0.0 442.5 jit_solution(3256196006250622005)
XLA Ops:
  7.2 0.7 broadcast_multiply_fusion
  8.0 0.8 copy.14
  9.3 0.6 reduce-window.6
  9.9 0.2 slice_reduce_fusion
  10.3 1.4 scatter_custom_fusion
  11.8 0.9 concatenate.3
  12.7 2.0 gather_fusion
  14.9 21.5 %all_to_all.10 = bf16[8,64,768]{2,1,0:T(8,128)(2,1)S(1)} all-to-all(bf16[8,64,768]{2,1,0:T(8,128)(2,1)S(1)} %broadcast_select_fusion), channel_id=1, replica_groups=mesh['section'=16,'expert'=8,'dp'=4] {'expert'}, dimensions={0} | all-to-all | bytes 1572864 | tf_op jit(solution)/shard_map/all_to_all | solution.py:23
  36.4 1.6 fusion.8
  38.1 1.6 fusion.12
  39.7 73.3 %all-reduce.4.cloned.1.call-done = (f32[512,512]{1,0:T(8,128)}, f32[512,512]{1,0:T(8,128)}) async-done(((f32[512,512]{1,0:T(8,128)}, f32[512,512]{1,0:T(8,128)}), (f32[512,512]{1,0:T(8,128)}, f32[512,512]{1,0:T(8,128)})) %all-reduce.4.cloned.1.call-update) | async-done | bytes 2097168 | tf_op jit(solution)/shard_map/psum | solution.py:32
  113.0 2.9 fusion.4
  115.9 0.8 copy-done.1
  116.7 0.6 fusion.10
  117.3 2.0 convolution_add_fusion
  119.4 274.4 %all-gather.3.cloned.1.call-done = f32[8192,768]{1,0:T(8,128)} async-done(((f32[512,768]{1,0:T(8,128)}), f32[8192,768]{1,0:T(8,128)}) %all-gather.3.cloned.1.call-update) | async-done | bytes 25165840 | tf_op jit(solution)/shard_map/all_gather | solution.py:47
  393.8 10.7 %reduce_sum.34 = f32[512,768]{1,0:T(8,128)} reduce(f32[16,512,768]{2,1,0:T(8,128)} %bitcast.45, f32[]{:T(128)} %constant.60.clone.1), dimensions={0}, to_apply=%region_6.7 | reduce | flops 5898240 | bytes 26738692 | tf_op jit(solution)/shard_map/reduce_sum | solution.py:47
  404.5 5.3 %all-to-all-start.1 = ((f32[8,64,768]{2,1,0:T(8,128)}), f32[8,64,768]{2,1,0:T(8,128)S(1)}, u32[]{:S(2)}, u32[]{:S(2)}) async-start(f32[8,64,768]{2,1,0:T(8,128)} %bitcast.50), calls=%async_computation.1 | async-start | bytes 3145728 | tf_op jit(solution)/shard_map/all_to_all | solution.py:48
  410.2 2.6 fusion
  412.8 1.6 fusion.1
  414.4 15.9 %all-to-all-done.1 = f32[8,64,768]{2,1,0:T(8,128)S(1)} async-done(((f32[8,64,768]{2,1,0:T(8,128)}), f32[8,64,768]{2,1,0:T(8,128)S(1)}, u32[]{:S(2)}, u32[]{:S(2)}) %all-to-all-start.1) | async-done | bytes 1572896 | tf_op jit(solution)/shard_map/all_to_all | solution.py:48
  430.3 2.0 gather_fusion.1
  432.3 1.6 gather.15
  433.9 1.8 select_reduce_fusion
  (39 shorter events, 1.4 us)
Async XLA Ops:
  7.2 30.9 %copy-start = (bf16[1,768,512]{2,1,0:T(8,128)(2,1)S(1)}, bf16[1,768,512]{2,1,0:T(8,128)(2,1)}, u32[]{:S(2)}) copy-start(bf16[1,768,512]{2,1,0:T(8,128)(2,1)} %param.7) | copy-start | bytes 2359300
  7.2 105.8 %all-reduce.4.cloned.1.call-start = ((), (), s32[]{:S(2)}) async-start(), calls=%async_computation.3 | async-start | bytes 4194304 | tf_op jit(solution)/shard_map/psum | solution.py:32
  14.8 21.7 %copy-start.4 = (bf16[1,768,512]{2,1,0:T(8,128)(2,1)S(1)}, bf16[1,768,512]{2,1,0:T(8,128)(2,1)}, u32[]{:S(2)}) copy-start(bf16[1,768,512]{2,1,0:T(8,128)(2,1)} %param.8) | copy-start | bytes 2359300
  39.6 73.4 %copy-start.5 = (bf16[1,512,512]{2,1,0:T(8,128)(2,1)S(1)}, bf16[1,512,512]{2,1,0:T(8,128)(2,1)}, u32[]{:S(2)}) copy-start(bf16[1,512,512]{2,1,0:T(8,128)(2,1)} %param.9) | copy-start | bytes 1572868
  39.6 354.2 %all-gather.3.cloned.1.call-start = ((), (), s32[]{:S(2)}) async-start(), calls=%async_computation.2 | async-start | bytes 26738688 | tf_op jit(solution)/shard_map/all_gather | solution.py:47
  115.9 0.8 copy-start.1
  115.9 1.4 copy-start.2
  404.5 5.5 %copy-start.7 = (s32[128,2]{0,1:T(2,128)S(1)}, s32[128,2]{0,1:T(2,128)}, u32[]{:S(2)}) copy-start(s32[128,2]{0,1:T(2,128)} %param.6) | copy-start | bytes 3076
  404.5 25.8 %all-to-all-start.1 = ((f32[8,64,768]{2,1,0:T(8,128)}), f32[8,64,768]{2,1,0:T(8,128)S(1)}, u32[]{:S(2)}, u32[]{:S(2)}) async-start(f32[8,64,768]{2,1,0:T(8,128)} %bitcast.50), calls=%async_computation.1 | async-start | bytes 3145728 | tf_op jit(solution)/shard_map/all_to_all | solution.py:48
  410.1 2.7 copy-start.3
  410.1 2.7 copy-start.6
Sparse Core Ops, SparseCore 0:
  39.8 73.2 all-reduce.3
  119.5 274.2 all-gather.2
